TPU v7x, 512 devices: a whole 4x8x8 slice. The times are simulated.
512 devices in a mesh: rows: 64 (over x, y, core), vec: 8 (over z).
Axes of the slice: x: 4, y: 8, z: 8, core: 2. Of those that a mesh axis runs over, the one named last changes fastest.
Arguments:
- vectors: float32 [64, 131072], P('vec', 'rows'), may hold values from -6 to 6
- damage: float32 [131072], P('rows')
- diag_blocks: bfloat16 [1024, 128, 128], P('rows')
- upper_blocks: bfloat16 [8192, 128, 128], P('rows'), may hold values from -0.5 to 0.5
- block_rows: int32 [8192], P('rows'), may hold values from 0 to 1023, as said below
- block_cols: int32 [8192], P('rows'), may hold values from 1 to 1023, as said below
- live_slots: int32 [64], P('rows'), may hold values from 64 to 128, as said below
Outputs:
- product: float32 [64, 131072], P('vec', 'rows')
- projected: float32 [64, 64], P('vec')
Inputs may be any that keep to these rules, and one draw needn't show every extreme that they name: `block_rows`: the slots of device d name block rows d * 16 to (d + 1) * 16 - 1; a slot whose column lies on another device names one of the last 6 of these. block_cols[s] is greater than block_rows[s], and block_cols[s] // 16 lies between d and d + 3 for a slot of device d; some slots reach d + 3. A column on device e other than d is one of the first 6 block rows of e. A pair may appear in several slots; their blocks add. `live_slots`: some device has all its slots stored.
All inputs are finite; a program needn't handle non-finite values.
Results may differ from a plain program's by a relative error of at most 0.0029.
Values may be sent and summed in bfloat16 or wider, within the bound.
No kernel may reach another device: no remote copies, remote signals or barrier semaphores. Data moves between devices by JAX's collectives and lax.ppermute only.
A program may use at most 64 MiB of HBM per device.

v0:
```python
import jax
import jax.numpy as jnp
from jax import lax
from jax.sharding import PartitionSpec as P

REACH = 4
RIM = 6
resid_eta = 0.001


def passed_along(array, axis, by):
    devices = lax.axis_size(axis)
    pairs = [(i, i + by) for i in range(devices) if 0 <= i + by < devices]
    return lax.ppermute(array, axis, pairs)


def on_device(vectors, damage, diag_blocks, upper_blocks, block_rows, block_cols, live_slots):
    vec_here, width = vectors.shape
    rb_here = diag_blocks.shape[0]
    block_size = diag_blocks.shape[1]
    slot_count = upper_blocks.shape[0]
    mine = lax.axis_index("rows")
    soft = jnp.sqrt((1.0 - damage) ** 2 + resid_eta)
    scaled = (vectors * soft[None, :]).astype(jnp.bfloat16).reshape(vec_here, rb_here, block_size)
    stored = (jnp.arange(slot_count) < live_slots[0]).astype(jnp.float32)
    local_rows = block_rows - mine * rb_here
    row_pick = (local_rows[:, None] == jnp.arange(rb_here)[None, :]).astype(jnp.float32) * stored[
        :, None
    ]
    own_rows = jnp.einsum(
        "vrb,sr->vsb", scaled, row_pick.astype(jnp.bfloat16), preferred_element_type=jnp.float32
    ).astype(jnp.bfloat16)
    accum = jnp.einsum("vrj,rij->vri", scaled, diag_blocks, preferred_element_type=jnp.float32)
    backward = jnp.einsum(
        "vsi,sij->vsj", own_rows, upper_blocks, preferred_element_type=jnp.float32
    )
    pieces = [scaled]
    for step in range(1, REACH):
        pieces.append(passed_along(scaled[:, :RIM], "rows", -step))
    window = jnp.concatenate(pieces, axis=1)
    relative = block_cols - mine * rb_here
    dev_step = relative // rb_here
    within = relative - dev_step * rb_here
    col_index = jnp.where(dev_step == 0, within, rb_here + (dev_step - 1) * RIM + within)
    span = window.shape[1]
    col_pick = (col_index[:, None] == jnp.arange(span)[None, :]).astype(jnp.float32) * stored[
        :, None
    ]
    far_cols = jnp.einsum(
        "vcb,sc->vsb", window, col_pick.astype(jnp.bfloat16), preferred_element_type=jnp.float32
    ).astype(jnp.bfloat16)
    forward = jnp.einsum("vsj,sij->vsi", far_cols, upper_blocks, preferred_element_type=jnp.float32)
    gathered = jnp.einsum("vsi,sr->vri", forward, row_pick, precision=lax.Precision.HIGHEST)
    spread = jnp.einsum("vsj,sc->vcj", backward, col_pick, precision=lax.Precision.HIGHEST)
    gathered, spread = (gathered, spread)
    accum = accum + gathered + spread[:, :rb_here]
    for step in range(1, REACH):
        low = rb_here + (step - 1) * RIM
        arrived = passed_along(spread[:, low : low + RIM], "rows", step)
        accum = accum.at[:, :RIM].add(arrived)
    product = soft[None, :] * accum.reshape(vec_here, width)
    partial_gram = jnp.dot(
        vectors,
        lax.all_gather(product.astype(jnp.bfloat16), "vec", axis=0, tiled=True)
        .astype(jnp.float32)
        .T,
        precision=lax.Precision.HIGHEST,
        preferred_element_type=jnp.float32,
    )
    total_dof = width * lax.axis_size("rows")
    projected = lax.psum(partial_gram, "rows") / total_dof
    return (product, projected)


def solution(mesh):
    return jax.shard_map(
        on_device,
        mesh=mesh,
        in_specs=(
            P("vec", "rows"),
            P("rows"),
            P("rows", None, None),
            P("rows", None, None),
            P("rows"),
            P("rows"),
            P("rows"),
        ),
        out_specs=(P("vec", "rows"), P("vec", None)),
        check_vma=False,
    )
```

profile of v0, /device:TPU:1, one launch (start us, length us, event | category | flops | bytes accessed | tf_op | source)
XLA Modules:
  0.0 186.2 jit_solution(1229719728883084545)
XLA Ops:
  0.6 0.0 copy-start
  0.6 0.8 add_sqrt_fusion
  1.4 0.9 fusion.16
  2.3 1.3 collective-permute-start.2
  3.6 1.3 collective-permute-start.1
  4.9 8.8 %collective-permute-start = (bf16[8,6,128]{2,0,1:T(8,128)(2,1)S(1)}, bf16[8,6,128]{2,0,1:T(8,128)(2,1)S(1)}, u32[]{:S(2)}, u32[]{:S(2)}) collective-permute-start(bf16[8,6,128]{2,0,1:T(8,128)(2,1)S(1)} %slice.91), channel_id=1, source_target_pairs={{8,0},{16,8},{24,16},{32,24},{40,32},{48,40},{56,48},{64,56},{72,6... | collective-permute-start | bytes 36872 | tf_op jit(solution)/shard_map/ppermute | solution.py:14
  14.3 0.0 copy-start.1
  14.3 0.8 broadcast_subtract_fusion
  15.2 0.8 compare_select_fusion
  16.0 0.3 fusion.17
  16.3 3.4 %fusion.12 = f32[128,8,128]{2,1,0:T(8,128)S(1)} fusion(bf16[128,128,128]{2,1,0:T(8,128)(2,1)} %param.16, bf16[128,8,128]{2,0,1:T(8,128)(2,1)S(1)} %fusion.17), kind=kOutput, calls=%fused_computation.15 | convolution fusion | flops 33554432 | bytes 4980736 | tf_op jit(solution)/shard_map/vsi,sij->vsj/dot_general | solution.py:34
  19.7 0.5 fusion.2
  20.1 0.0 copy-start.2
  20.2 6.0 %collective-permute-start.5 = (f32[8,6,128]{2,0,1:T(8,128)S(1)}, f32[8,6,128]{2,0,1:T(8,128)S(1)}, u32[]{:S(2)}, u32[]{:S(2)}) collective-permute-start(f32[8,6,128]{2,0,1:T(8,128)S(1)} %get-tuple-element.40), channel_id=1, source_target_pairs={{0,24},{8,32},{16,40},{24,48},{32,56},{40,64},{48,72},{56,80},{64,... | collective-permute-start | bytes 73736 | tf_op jit(solution)/shard_map/ppermute | solution.py:14
  26.2 3.4 %collective-permute-start.4 = (f32[8,6,128]{2,0,1:T(8,128)S(1)}, f32[8,6,128]{2,0,1:T(8,128)S(1)}, u32[]{:S(2)}, u32[]{:S(2)}) collective-permute-start(f32[8,6,128]{2,0,1:T(8,128)S(1)} %get-tuple-element.41), channel_id=1, source_target_pairs={{0,16},{8,24},{16,32},{24,40},{32,48},{40,56},{48,64},{56,72},{64,... | collective-permute-start | bytes 73736 | tf_op jit(solution)/shard_map/ppermute | solution.py:14
  29.5 0.0 collective-permute-done.2
  29.5 1.9 %collective-permute-start.3 = (f32[8,6,128]{2,0,1:T(8,128)S(1)}, f32[8,6,128]{2,0,1:T(8,128)S(1)}, u32[]{:S(2)}, u32[]{:S(2)}) collective-permute-start(f32[8,6,128]{2,0,1:T(8,128)S(1)} %get-tuple-element.42), channel_id=1, source_target_pairs={{0,8},{8,16},{16,24},{24,32},{32,40},{40,48},{48,56},{56,64},{64,7... | collective-permute-start | bytes 73736 | tf_op jit(solution)/shard_map/ppermute | solution.py:14
  31.5 0.0 collective-permute-done.1
  31.5 0.0 collective-permute-done
  31.5 0.3 fusion.14
  31.8 0.0 copy-done.1
  31.8 2.3 %fusion.9 = f32[128,8,128]{2,1,0:T(8,128)S(1)} fusion(bf16[128,128,128]{2,1,0:T(8,128)(2,1)S(1)} %copy-done.1, bf16[128,8,128]{2,0,1:T(8,128)(2,1)S(1)} %fusion.14), kind=kOutput, calls=%fused_computation.13 | convolution fusion | flops 33554432 | bytes 4980736 | tf_op jit(solution)/shard_map/vsj,sij->vsi/dot_general | solution.py:52
  34.0 0.4 fusion.4
  34.5 0.0 copy-done
  34.5 0.4 fusion.1
  34.9 0.0 collective-permute-done.3
  34.9 0.0 collective-permute-done.4
  34.9 0.0 collective-permute-done.5
  34.9 0.6 fusion.39
  35.6 20.4 %all_gather.3 = bf16[64,2048]{1,0:T(8,128)(2,1)S(1)} all-gather(bf16[8,2048]{1,0:T(8,128)(2,1)S(1)} %get-tuple-element.38), channel_id=1, replica_groups=mesh['rows'=64,'vec'=8] {'vec'}, dimensions={0}, use_global_device_ids=true | all-gather | bytes 294912 | tf_op jit(solution)/shard_map/all_gather | solution.py:64
  56.0 0.0 copy-done.2
  56.0 0.3 convolution_bitcast_fusion
  56.3 129.3 %psum.7 = f32[8,64]{1,0:T(8,128)S(1)} all-reduce(f32[8,64]{1,0:T(8,128)S(1)} %convolution_bitcast_fusion), channel_id=1, replica_groups=mesh['rows'=64,'vec'=8] {'rows'}, use_global_device_ids=true, to_apply=%region_0.1 | all-reduce | flops 512 | bytes 4096 | tf_op jit(solution)/shard_map/psum | solution.py:71
  185.6 0.6 broadcast_multiply_fusion
  (9 shorter events, 0.1 us)
Async XLA Ops:
  0.6 33.8 %copy-start = (bf16[16,128,128]{2,1,0:T(8,128)(2,1)S(1)}, bf16[16,128,128]{2,1,0:T(8,128)(2,1)}, u32[]{:S(2)}) copy-start(bf16[16,128,128]{2,1,0:T(8,128)(2,1)} %param.15) | copy-start | bytes 1572868
  2.3 27.2 %collective-permute-start.2 = (bf16[8,6,128]{2,0,1:T(8,128)(2,1)S(1)}, bf16[8,6,128]{2,0,1:T(8,128)(2,1)S(1)}, u32[]{:S(2)}, u32[]{:S(2)}) collective-permute-start(bf16[8,6,128]{2,0,1:T(8,128)(2,1)S(1)} %slice.91), channel_id=1, source_target_pairs={{24,0},{32,8},{40,16},{48,24},{56,32},{64,40},{72,48},{80,56},{88,... | collective-permute-start | bytes 36872 | tf_op jit(solution)/shard_map/ppermute | solution.py:14
  3.6 27.9 %collective-permute-start.1 = (bf16[8,6,128]{2,0,1:T(8,128)(2,1)S(1)}, bf16[8,6,128]{2,0,1:T(8,128)(2,1)S(1)}, u32[]{:S(2)}, u32[]{:S(2)}) collective-permute-start(bf16[8,6,128]{2,0,1:T(8,128)(2,1)S(1)} %slice.91), channel_id=1, source_target_pairs={{16,0},{24,8},{32,16},{40,24},{48,32},{56,40},{64,48},{72,56},{80,... | collective-permute-start | bytes 36872 | tf_op jit(solution)/shard_map/ppermute | solution.py:14
  4.9 26.6 %collective-permute-start = (bf16[8,6,128]{2,0,1:T(8,128)(2,1)S(1)}, bf16[8,6,128]{2,0,1:T(8,128)(2,1)S(1)}, u32[]{:S(2)}, u32[]{:S(2)}) collective-permute-start(bf16[8,6,128]{2,0,1:T(8,128)(2,1)S(1)} %slice.91), channel_id=1, source_target_pairs={{8,0},{16,8},{24,16},{32,24},{40,32},{48,40},{56,48},{64,56},{72,6... | collective-permute-start | bytes 36872 | tf_op jit(solution)/shard_map/ppermute | solution.py:14
  14.3 17.4 %copy-start.1 = (bf16[128,128,128]{2,1,0:T(8,128)(2,1)S(1)}, bf16[128,128,128]{2,1,0:T(8,128)(2,1)}, u32[]{:S(2)}) copy-start(bf16[128,128,128]{2,1,0:T(8,128)(2,1)} %param.16) | copy-start | bytes 12582916
  20.1 35.9 %copy-start.2 = (f32[8,2048]{1,0:T(8,128)S(1)}, f32[8,2048]{1,0:T(8,128)}, u32[]{:S(2)}) copy-start(f32[8,2048]{1,0:T(8,128)} %param.13) | copy-start | bytes 196612
  20.2 14.7 %collective-permute-start.5 = (f32[8,6,128]{2,0,1:T(8,128)S(1)}, f32[8,6,128]{2,0,1:T(8,128)S(1)}, u32[]{:S(2)}, u32[]{:S(2)}) collective-permute-start(f32[8,6,128]{2,0,1:T(8,128)S(1)} %get-tuple-element.40), channel_id=1, source_target_pairs={{0,24},{8,32},{16,40},{24,48},{32,56},{40,64},{48,72},{56,80},{64,... | collective-permute-start | bytes 73736 | tf_op jit(solution)/shard_map/ppermute | solution.py:14
  26.2 8.7 %collective-permute-start.4 = (f32[8,6,128]{2,0,1:T(8,128)S(1)}, f32[8,6,128]{2,0,1:T(8,128)S(1)}, u32[]{:S(2)}, u32[]{:S(2)}) collective-permute-start(f32[8,6,128]{2,0,1:T(8,128)S(1)} %get-tuple-element.41), channel_id=1, source_target_pairs={{0,16},{8,24},{16,32},{24,40},{32,48},{40,56},{48,64},{56,72},{64,... | collective-permute-start | bytes 73736 | tf_op jit(solution)/shard_map/ppermute | solution.py:14
  29.5 5.3 %collective-permute-start.3 = (f32[8,6,128]{2,0,1:T(8,128)S(1)}, f32[8,6,128]{2,0,1:T(8,128)S(1)}, u32[]{:S(2)}, u32[]{:S(2)}) collective-permute-start(f32[8,6,128]{2,0,1:T(8,128)S(1)} %get-tuple-element.42), channel_id=1, source_target_pairs={{0,8},{8,16},{16,24},{24,32},{32,40},{40,48},{48,56},{56,64},{64,7... | collective-permute-start | bytes 73736 | tf_op jit(solution)/shard_map/ppermute | solution.py:14
where the time goes:
time: 187 us; the launch traced here: 186 us
  blocking collectives  150 us (80%)
  starting transfers between devices  22.6 us (12%)
  matrix products  7.72 us (4%)
  other arithmetic  4.55 us (2%)
    psum x1, blocking collectives, on_device(): projected = lax.psum(partial_gram, 'rows') / total_dof  129 us
    ppermute x6, starting transfers between devices, passed_along(): return lax.ppermute(array, axis, pairs)  22.6 us
    all_gather x1, blocking collectives, on_device(): lax.all_gather(product.astype(jnp.bfloat16), 'vec', axis=0, tiled=True)  20.4 us
  transfers between devices with their start and end apart: 6, of which 0 were waited for; matrix products, arithmetic and copies ran while one was open for 5% of the time, Pallas kernels for 0%

commit v1 on v0

--- a/solution.py
+++ b/solution.py
@@ -61,7 +61,12 @@
     product = soft[None, :] * accum.reshape(vec_here, width)
     partial_gram = jnp.dot(
         vectors,
-        lax.all_gather(product.astype(jnp.bfloat16), "vec", axis=0, tiled=True)
+        jnp.concatenate(
+            lax.all_to_all(
+                jnp.stack([product.astype(jnp.bfloat16)] * lax.axis_size("vec")), "vec", 0, 0
+            ),
+            axis=0,
+        )
         .astype(jnp.float32)
         .T,
         precision=lax.Precision.HIGHEST,

time: 187 us -> 178 us (0.952)
  blocking collectives: 150 us -> 141 us
    all_gather x1 -> x0, blocking collectives: 20.4 us -> none  [on_device(): lax.all_gather(product.astype(jnp.bfloat16), 'vec', axis=0, tiled=True)]
    all_to_all x0 -> x1, blocking collectives: none -> 17.5 us  [on_device(): lax.all_to_all(jnp.stack([product.astype(jnp.bfloat16)] * lax.axis_size('...]
    psum x1, blocking collectives: 129 us -> 124 us  [on_device(): projected = lax.psum(partial_gram, 'rows') / total_dof]
where the time goes in v1:
time: 178 us
  blocking collectives  141 us (79%)
  starting transfers between devices  22.6 us (13%)
  matrix products  7.72 us (4%)
  other arithmetic  4.55 us (3%)
    psum x1, blocking collectives, on_device(): projected = lax.psum(partial_gram, 'rows') / total_dof  124 us
    ppermute x6, starting transfers between devices, passed_along(): return lax.ppermute(array, axis, pairs)  22.6 us
    all_to_all x1, blocking collectives, on_device(): lax.all_to_all(jnp.stack([product.astype(jnp.bfloat16)] * lax.axis_size('...  17.5 us
  transfers between devices with their start and end apart: 6, of which 0 were waited for; matrix products, arithmetic and copies ran while one was open for 5% of the time, Pallas kernels for 0%

profile of v1, /device:TPU:1, one launch (start us, length us, event | category | flops | bytes accessed | tf_op | source)
XLA Modules:
  0.0 177.8 jit_solution(8539367013519874851)
XLA Ops:
  0.6 0.0 copy-start
  0.6 0.8 add_sqrt_fusion
  1.4 0.9 fusion.17
  2.3 1.3 collective-permute-start.2
  3.6 1.3 collective-permute-start.1
  4.9 8.8 %collective-permute-start = (bf16[8,6,128]{2,0,1:T(8,128)(2,1)S(1)}, bf16[8,6,128]{2,0,1:T(8,128)(2,1)S(1)}, u32[]{:S(2)}, u32[]{:S(2)}) collective-permute-start(bf16[8,6,128]{2,0,1:T(8,128)(2,1)S(1)} %slice.91), channel_id=1, source_target_pairs={{8,0},{16,8},{24,16},{32,24},{40,32},{48,40},{56,48},{64,56},{72,6... | collective-permute-start | bytes 36872 | tf_op jit(solution)/shard_map/ppermute | solution.py:14
  14.3 0.0 copy-start.1
  14.3 0.8 broadcast_subtract_fusion
  15.2 0.8 compare_select_fusion
  16.0 0.3 fusion.18
  16.3 3.4 %fusion.12 = f32[128,8,128]{2,1,0:T(8,128)S(1)} fusion(bf16[128,128,128]{2,1,0:T(8,128)(2,1)} %param.16, bf16[128,8,128]{2,0,1:T(8,128)(2,1)S(1)} %fusion.18), kind=kOutput, calls=%fused_computation.15 | convolution fusion | flops 33554432 | bytes 4980736 | tf_op jit(solution)/shard_map/vsi,sij->vsj/dot_general | solution.py:34
  19.7 0.5 fusion.2
  20.2 0.0 copy-start.2
  20.2 6.0 %collective-permute-start.5 = (f32[8,6,128]{2,0,1:T(8,128)S(1)}, f32[8,6,128]{2,0,1:T(8,128)S(1)}, u32[]{:S(2)}, u32[]{:S(2)}) collective-permute-start(f32[8,6,128]{2,0,1:T(8,128)S(1)} %get-tuple-element.40), channel_id=1, source_target_pairs={{0,24},{8,32},{16,40},{24,48},{32,56},{40,64},{48,72},{56,80},{64,... | collective-permute-start | bytes 73736 | tf_op jit(solution)/shard_map/ppermute | solution.py:14
  26.2 3.4 %collective-permute-start.4 = (f32[8,6,128]{2,0,1:T(8,128)S(1)}, f32[8,6,128]{2,0,1:T(8,128)S(1)}, u32[]{:S(2)}, u32[]{:S(2)}) collective-permute-start(f32[8,6,128]{2,0,1:T(8,128)S(1)} %get-tuple-element.41), channel_id=1, source_target_pairs={{0,16},{8,24},{16,32},{24,40},{32,48},{40,56},{48,64},{56,72},{64,... | collective-permute-start | bytes 73736 | tf_op jit(solution)/shard_map/ppermute | solution.py:14
  29.5 0.0 collective-permute-done.2
  29.5 1.9 %collective-permute-start.3 = (f32[8,6,128]{2,0,1:T(8,128)S(1)}, f32[8,6,128]{2,0,1:T(8,128)S(1)}, u32[]{:S(2)}, u32[]{:S(2)}) collective-permute-start(f32[8,6,128]{2,0,1:T(8,128)S(1)} %get-tuple-element.42), channel_id=1, source_target_pairs={{0,8},{8,16},{16,24},{24,32},{32,40},{40,48},{48,56},{56,64},{64,7... | collective-permute-start | bytes 73736 | tf_op jit(solution)/shard_map/ppermute | solution.py:14
  31.5 0.0 collective-permute-done.1
  31.5 0.0 collective-permute-done
  31.5 0.3 fusion.15
  31.8 0.0 copy-done.1
  31.8 2.3 %fusion.9 = f32[128,8,128]{2,1,0:T(8,128)S(1)} fusion(bf16[128,128,128]{2,1,0:T(8,128)(2,1)S(1)} %copy-done.1, bf16[128,8,128]{2,0,1:T(8,128)(2,1)S(1)} %fusion.15), kind=kOutput, calls=%fused_computation.13 | convolution fusion | flops 33554432 | bytes 4980736 | tf_op jit(solution)/shard_map/vsj,sij->vsi/dot_general | solution.py:52
  34.0 0.4 fusion.4
  34.5 0.0 copy-done
  34.5 0.4 fusion.1
  34.9 0.0 collective-permute-done.3
  34.9 0.0 collective-permute-done.4
  34.9 0.0 collective-permute-done.5
  34.9 0.6 fusion.40
  35.6 17.5 %all_to_all.5 = bf16[8,8,2048]{2,1,0:T(8,128)(2,1)S(1)} all-to-all(bf16[8,8,2048]{2,1,0:T(8,128)(2,1)S(1)} %stack.2), channel_id=1, replica_groups=mesh['rows'=64,'vec'=8] {'vec'}, dimensions={0} | all-to-all | bytes 524288 | tf_op jit(solution)/shard_map/all_to_all | solution.py:65
  53.1 0.0 copy-done.2
  53.1 0.3 convolution_bitcast_fusion
  53.4 123.9 %psum.7 = f32[8,64]{1,0:T(8,128)S(1)} all-reduce(f32[8,64]{1,0:T(8,128)S(1)} %convolution_bitcast_fusion), channel_id=1, replica_groups=mesh['rows'=64,'vec'=8] {'rows'}, use_global_device_ids=true, to_apply=%region_0.1 | all-reduce | flops 512 | bytes 4096 | tf_op jit(solution)/shard_map/psum | solution.py:76
  177.2 0.6 broadcast_multiply_fusion
  (10 shorter events, 0.1 us)
Async XLA Ops:
  0.6 33.8 %copy-start = (bf16[16,128,128]{2,1,0:T(8,128)(2,1)S(1)}, bf16[16,128,128]{2,1,0:T(8,128)(2,1)}, u32[]{:S(2)}) copy-start(bf16[16,128,128]{2,1,0:T(8,128)(2,1)} %param.15) | copy-start | bytes 1572868
  2.3 27.2 %collective-permute-start.2 = (bf16[8,6,128]{2,0,1:T(8,128)(2,1)S(1)}, bf16[8,6,128]{2,0,1:T(8,128)(2,1)S(1)}, u32[]{:S(2)}, u32[]{:S(2)}) collective-permute-start(bf16[8,6,128]{2,0,1:T(8,128)(2,1)S(1)} %slice.91), channel_id=1, source_target_pairs={{24,0},{32,8},{40,16},{48,24},{56,32},{64,40},{72,48},{80,56},{88,... | collective-permute-start | bytes 36872 | tf_op jit(solution)/shard_map/ppermute | solution.py:14
  3.6 27.9 %collective-permute-start.1 = (bf16[8,6,128]{2,0,1:T(8,128)(2,1)S(1)}, bf16[8,6,128]{2,0,1:T(8,128)(2,1)S(1)}, u32[]{:S(2)}, u32[]{:S(2)}) collective-permute-start(bf16[8,6,128]{2,0,1:T(8,128)(2,1)S(1)} %slice.91), channel_id=1, source_target_pairs={{16,0},{24,8},{32,16},{40,24},{48,32},{56,40},{64,48},{72,56},{80,... | collective-permute-start | bytes 36872 | tf_op jit(solution)/shard_map/ppermute | solution.py:14
  4.9 26.6 %collective-permute-start = (bf16[8,6,128]{2,0,1:T(8,128)(2,1)S(1)}, bf16[8,6,128]{2,0,1:T(8,128)(2,1)S(1)}, u32[]{:S(2)}, u32[]{:S(2)}) collective-permute-start(bf16[8,6,128]{2,0,1:T(8,128)(2,1)S(1)} %slice.91), channel_id=1, source_target_pairs={{8,0},{16,8},{24,16},{32,24},{40,32},{48,40},{56,48},{64,56},{72,6... | collective-permute-start | bytes 36872 | tf_op jit(solution)/shard_map/ppermute | solution.py:14
  14.3 17.4 %copy-start.1 = (bf16[128,128,128]{2,1,0:T(8,128)(2,1)S(1)}, bf16[128,128,128]{2,1,0:T(8,128)(2,1)}, u32[]{:S(2)}) copy-start(bf16[128,128,128]{2,1,0:T(8,128)(2,1)} %param.16) | copy-start | bytes 12582916
  20.2 32.9 %copy-start.2 = (f32[8,2048]{1,0:T(8,128)S(1)}, f32[8,2048]{1,0:T(8,128)}, u32[]{:S(2)}) copy-start(f32[8,2048]{1,0:T(8,128)} %param.13) | copy-start | bytes 196612
  20.2 14.7 %collective-permute-start.5 = (f32[8,6,128]{2,0,1:T(8,128)S(1)}, f32[8,6,128]{2,0,1:T(8,128)S(1)}, u32[]{:S(2)}, u32[]{:S(2)}) collective-permute-start(f32[8,6,128]{2,0,1:T(8,128)S(1)} %get-tuple-element.40), channel_id=1, source_target_pairs={{0,24},{8,32},{16,40},{24,48},{32,56},{40,64},{48,72},{56,80},{64,... | collective-permute-start | bytes 73736 | tf_op jit(solution)/shard_map/ppermute | solution.py:14
  26.2 8.7 %collective-permute-start.4 = (f32[8,6,128]{2,0,1:T(8,128)S(1)}, f32[8,6,128]{2,0,1:T(8,128)S(1)}, u32[]{:S(2)}, u32[]{:S(2)}) collective-permute-start(f32[8,6,128]{2,0,1:T(8,128)S(1)} %get-tuple-element.41), channel_id=1, source_target_pairs={{0,16},{8,24},{16,32},{24,40},{32,48},{40,56},{48,64},{56,72},{64,... | collective-permute-start | bytes 73736 | tf_op jit(solution)/shard_map/ppermute | solution.py:14
  29.5 5.3 %collective-permute-start.3 = (f32[8,6,128]{2,0,1:T(8,128)S(1)}, f32[8,6,128]{2,0,1:T(8,128)S(1)}, u32[]{:S(2)}, u32[]{:S(2)}) collective-permute-start(f32[8,6,128]{2,0,1:T(8,128)S(1)} %get-tuple-element.42), channel_id=1, source_target_pairs={{0,8},{8,16},{16,24},{24,32},{32,40},{40,48},{48,56},{56,64},{64,7... | collective-permute-start | bytes 73736 | tf_op jit(solution)/shard_map/ppermute | solution.py:14
